TPU v7x, 512 devices: a whole 4x8x8 slice. The times are simulated.
512 devices in a mesh: fsdp: 16 (over y, core), ctx: 32 (over z, x).
Axes of the slice: x: 4, y: 8, z: 8, core: 2. Of those that a mesh axis runs over, the one named last changes fastest.
Arguments:
- featurized: bfloat16 [4096, 3, 4096], P('ctx', None, 'fsdp'), may hold values from -6 to 6
- short_taps: float32 [3, 3, 4096], P(None, None, 'fsdp'), may hold values from -3 to 3
- residues: float32 [4096, 16], P('fsdp'), may hold values from -1.5 to 1.5
- decay_rates: float32 [4096, 16], P('fsdp'), may hold values from 0.00012207031 to 0.05
- w_out: bfloat16 [4096, 8192], P('fsdp', 'ctx'), may hold values from -0.09375 to 0.09375
- grad_out: bfloat16 [4096, 8192], P('ctx'), may hold values from -6 to 6
Outputs:
- block_output: bfloat16 [4096, 8192], P('ctx', 'fsdp')
- grad_features: bfloat16 [4096, 3, 4096], P('ctx', None, 'fsdp')
All inputs are finite; a program needn't handle non-finite values.
Results may differ from a plain program's by a relative error of at most 0.02.
Values may be sent and summed in bfloat16 or wider, within the bound.
A program may use at most 64 MiB of HBM per device.

v0:
```python
import math
import jax
import jax.numpy as jnp
from jax import lax
from jax.sharding import PartitionSpec as P

HIGHEST = lax.Precision.HIGHEST


def swapped(block, axis, distance):
    count = lax.axis_size(axis)
    route = []
    for low in range(count):
        high = low | 1 << distance
        if high != low and high < count:
            route += [(low, high), (high, low)]
    return lax.ppermute(block, axis, route)


def shifted(block, axis, distance):
    devices = range(lax.axis_size(axis))
    route = [(i - distance, i) for i in devices if i - distance in devices]
    return lax.ppermute(block, axis, route)


def angles(product_index, modulus):
    phases = (product_index % modulus).astype(jnp.float32) * (2.0 * math.pi / modulus)
    return (jnp.cos(phases), jnp.sin(phases))


def complex_contract(pattern, table_re, table_im, real_part, imag_part):
    first_term = jnp.einsum(pattern, table_re, real_part, precision=HIGHEST)
    second_term = jnp.einsum(pattern, table_im, imag_part, precision=HIGHEST)
    third_term = jnp.einsum(pattern, table_re, imag_part, precision=HIGHEST)
    fourth_term = jnp.einsum(pattern, table_im, real_part, precision=HIGHEST)
    return (first_term - second_term, third_term + fourth_term)


def token_tables(tokens_here):
    positions_all = jnp.arange(tokens_here)
    return angles(positions_all[:, None] * positions_all[None, :], tokens_here)


def reversed_bits(my_rank, bit_count):
    result = jnp.zeros((), jnp.int32)
    for section_bit in range(bit_count):
        result = result + (my_rank >> section_bit & 1) * (1 << bit_count - 1 - section_bit)
    return result


def partner_step(values_now, section_bit, my_rank, inverse):
    partner_data = swapped(values_now.astype(jnp.bfloat16), "ctx", section_bit).astype(
        values_now.dtype
    )
    half_span = 1 << section_bit
    upper_side = my_rank >> section_bit & 1 == 1
    cos_turn, sin_turn = angles(my_rank % half_span, 2 * half_span)
    if inverse:
        spun_re = partner_data[0] * cos_turn - partner_data[1] * sin_turn
        spun_im = partner_data[1] * cos_turn + partner_data[0] * sin_turn
        lower_new = jnp.stack([values_now[0] + spun_re, values_now[1] + spun_im]) * 0.5
        mine_re = values_now[0] * cos_turn - values_now[1] * sin_turn
        mine_im = values_now[1] * cos_turn + values_now[0] * sin_turn
        upper_new = jnp.stack([partner_data[0] - mine_re, partner_data[1] - mine_im]) * 0.5
    else:
        lower_new = values_now + partner_data
        differ = partner_data - values_now
        upper_new = jnp.stack(
            [
                differ[0] * cos_turn + differ[1] * sin_turn,
                differ[1] * cos_turn - differ[0] * sin_turn,
            ]
        )
    return jnp.where(upper_side, upper_new, lower_new)


def forward_partners(signal):
    tokens_here = signal.shape[0]
    devices = lax.axis_size("ctx")
    bit_count = devices.bit_length() - 1
    my_rank = lax.axis_index("ctx")
    full_length = 2 * devices * tokens_here
    half_turn = my_rank.astype(jnp.float32) * (math.pi / devices)
    values_now = jnp.stack(
        [
            jnp.stack([signal, signal * jnp.cos(half_turn)]),
            jnp.stack([jnp.zeros_like(signal), -signal * jnp.sin(half_turn)]),
        ]
    )
    for section_bit in reversed(range(bit_count)):
        values_now = partner_step(values_now, section_bit, my_rank, False)
    spectral_rows = 2 * reversed_bits(my_rank, bit_count) + jnp.arange(2)
    cos_twist, sin_twist = angles(
        spectral_rows[:, None] * jnp.arange(tokens_here)[None, :], full_length
    )
    cos_twist = cos_twist[:, :, None, None]
    sin_twist = sin_twist[:, :, None, None]
    twist_re = values_now[0] * cos_twist + values_now[1] * sin_twist
    twist_im = values_now[1] * cos_twist - values_now[0] * sin_twist
    cos_tokens, sin_tokens = token_tables(tokens_here)
    return complex_contract("ks,esgc->ekgc", cos_tokens, -sin_tokens, twist_re, twist_im)


def inverse_partners(spec_re, spec_im):
    tokens_here = spec_re.shape[1]
    devices = lax.axis_size("ctx")
    bit_count = devices.bit_length() - 1
    my_rank = lax.axis_index("ctx")
    full_length = 2 * devices * tokens_here
    cos_tokens, sin_tokens = token_tables(tokens_here)
    plain_re, plain_im = complex_contract("sk,ekgc->esgc", cos_tokens, sin_tokens, spec_re, spec_im)
    spectral_rows = 2 * reversed_bits(my_rank, bit_count) + jnp.arange(2)
    cos_twist, sin_twist = angles(
        spectral_rows[:, None] * jnp.arange(tokens_here)[None, :], full_length
    )
    cos_twist = cos_twist[:, :, None, None]
    sin_twist = sin_twist[:, :, None, None]
    twist_re = plain_re * cos_twist - plain_im * sin_twist
    twist_im = plain_re * sin_twist + plain_im * cos_twist
    values_now = jnp.stack([twist_re, twist_im])
    for section_bit in range(bit_count):
        values_now = partner_step(values_now, section_bit, my_rank, True)
    half_turn = my_rank.astype(jnp.float32) * (math.pi / devices)
    real_part = (
        values_now[0, 0]
        + values_now[0, 1] * jnp.cos(half_turn)
        - values_now[1, 1] * jnp.sin(half_turn)
    )
    return real_part / (2.0 * tokens_here)


def to_spectrum(signal):
    return forward_partners(signal)


def from_spectrum(spec_re, spec_im):
    return inverse_partners(spec_re, spec_im)


def modal_spectrum(residues, decay_rates, spectral_rows, tokens_here, devices):
    full_length = 2 * devices * tokens_here
    sequence = devices * tokens_here
    frequency = spectral_rows[:, None] + 2 * devices * jnp.arange(tokens_here)[None, :]
    angle_now = frequency.astype(jnp.float32) * (math.pi / full_length)
    half_sine = jnp.sin(angle_now)[:, :, None]
    full_sine = jnp.sin(2.0 * angle_now)[:, :, None]
    parity_sign = (1 - 2 * (spectral_rows % 2)).astype(jnp.float32)[:, None, None]

    def add_mode(mode_index, totals):
        rates_now = lax.dynamic_slice_in_dim(decay_rates, mode_index, 1, 1)[:, 0]
        weight = lax.dynamic_slice_in_dim(residues, mode_index, 1, 1)[:, 0] * jnp.sqrt(rates_now)
        decay_now = jnp.exp(-rates_now)
        numerator = 1.0 - parity_sign * jnp.exp(-rates_now * sequence)
        denom_re = -jnp.expm1(-rates_now) + 2.0 * decay_now * half_sine * half_sine
        denom_im = decay_now * full_sine
        scaled = weight * numerator / (denom_re * denom_re + denom_im * denom_im)
        return (totals[0] + scaled * denom_re, totals[1] - scaled * denom_im)

    empty = jnp.zeros((spectral_rows.shape[0], tokens_here, residues.shape[0]), jnp.float32)
    spec_re, spec_im = lax.fori_loop(0, residues.shape[1], add_mode, (empty, empty))
    return (spec_re[:, :, None, :], spec_im[:, :, None, :])


def own_filter(residues, decay_rates, tokens_here):
    devices = lax.axis_size("ctx")
    my_rank = lax.axis_index("ctx")
    pair_rank = reversed_bits(my_rank, devices.bit_length() - 1)
    return modal_spectrum(
        residues, decay_rates, 2 * pair_rank + jnp.arange(2), tokens_here, devices
    )


def per_device(featurized, short_taps, residues, decay_rates, w_out, grad_out):
    tokens_here = featurized.shape[0]
    before = shifted(featurized[tokens_here - 2 :], "ctx", 1)
    raw_values = featurized.astype(jnp.float32)
    extended = jnp.concatenate([before.astype(jnp.float32), raw_values], axis=0)
    mixed_in = (
        short_taps[0] * extended[2:]
        + short_taps[1] * extended[1 : tokens_here + 1]
        + short_taps[2] * extended[:tokens_here]
    )
    query_part = mixed_in[:, 0]
    key_part = mixed_in[:, 1]
    value_part = mixed_in[:, 2]
    carried = key_part * value_part
    signal_re, signal_im = to_spectrum(carried[:, None, :])
    filter_re, filter_im = own_filter(residues, decay_rates, tokens_here)
    conv_re = signal_re * filter_re - signal_im * filter_im
    conv_im = signal_re * filter_im + signal_im * filter_re
    convolved = from_spectrum(conv_re, conv_im)[:, 0]
    gated_out = (query_part * convolved).astype(jnp.bfloat16)
    w_full = lax.all_gather(w_out, "ctx", axis=1, tiled=True)
    partial_sum = jnp.dot(gated_out, w_full, preferred_element_type=jnp.float32)
    block_output = lax.psum_scatter(
        partial_sum.astype(jnp.bfloat16), "fsdp", scatter_dimension=1, tiled=True
    )
    grad_gated = lax.dot_general(
        grad_out, w_full, (((1,), (1,)), ((), ())), preferred_element_type=jnp.float32
    )
    grad_query = grad_gated * convolved
    grad_conv = grad_gated * query_part
    delta_re, delta_im = to_spectrum(grad_conv[:, None, :])
    back_re = filter_re * delta_re + filter_im * delta_im
    back_im = filter_re * delta_im - filter_im * delta_re
    grad_carried = from_spectrum(back_re, back_im)[:, 0]
    grad_mixed = jnp.stack([grad_query, grad_carried * value_part, grad_carried * key_part], axis=1)
    following = shifted(grad_mixed[:2], "ctx", -1)
    padded = jnp.concatenate([grad_mixed, following], axis=0)
    grad_features = (
        short_taps[0] * padded[:tokens_here]
        + short_taps[1] * padded[1 : tokens_here + 1]
        + short_taps[2] * padded[2:]
    ).astype(jnp.bfloat16)
    return (block_output, grad_features)


def solution(mesh):
    placed = (
        P("ctx", None, "fsdp"),
        P(None, None, "fsdp"),
        P("fsdp", None),
        P("fsdp", None),
        P("fsdp", "ctx"),
        P("ctx", None),
    )
    return jax.shard_map(
        per_device,
        mesh=mesh,
        in_specs=placed,
        out_specs=(P("ctx", "fsdp"), P("ctx", None, "fsdp")),
        check_vma=False,
    )
```

profile of v0, /device:TPU:25, one launch (start us, length us, event | category | flops | bytes accessed | tf_op | source)
XLA Modules:
  0.0 354.1 jit_solution(11547537968246586453)
XLA Ops:
  8.7 3.1 collective-permute-start
  15.2 12.7 %collective-permute-start.1 = (bf16[2,2,128,1,256]{4,2,1,3,0:T(8,128)(2,1)}, bf16[2,2,128,1,256]{4,2,1,3,0:T(8,128)(2,1)}, u32[]{:S(2)}, u32[]{:S(2)}) collective-permute-start(bf16[2,2,128,1,256]{4,2,1,3,0:T(8,128)(2,1)} %fusion.53), channel_id=1, source_target_pairs={{0,16},{16,0},{1,17},{17,1},{2,18},{18,2},{3,19},{19,3},{4,20},{20... | collective-permute-start | bytes 786440 | tf_op jit(solution)/shard_map/ppermute | solution.py:17
  27.9 78.2 %all-gather.2.cloned.1.call-done = bf16[256,8192]{1,0:T(8,128)(2,1)} async-done(((bf16[256,256]{1,0:T(8,128)(2,1)}), bf16[256,8192]{1,0:T(8,128)(2,1)}) %all-gather.2.cloned.1.call-update) | async-done | bytes 4194320 | tf_op jit(solution)/shard_map/all_gather | solution.py:193
  106.1 3.7 %fusion.254 = f32[128,256]{1,0:T(8,128)S(1)} fusion(bf16[128,8192]{1,0:T(8,128)(2,1)S(1)} %copy-done, bf16[256,8192]{1,0:T(8,128)(2,1)} %all-gather.2.cloned.1.call-done), kind=kOutput, calls=%fused_computation.407 | convolution fusion | flops 536870912 | bytes 6422528 | tf_op jit(solution)/shard_map/dot_general | solution.py:198
  110.5 4.2 %collective-permute-start.11 = (bf16[2,2,128,1,256]{4,2,1,3,0:T(8,128)(2,1)S(1)}, bf16[2,2,128,1,256]{4,2,1,3,0:T(8,128)(2,1)S(1)}, u32[]{:S(2)}, u32[]{:S(2)}) collective-permute-start(bf16[2,2,128,1,256]{4,2,1,3,0:T(8,128)(2,1)S(1)} %fusion.52), channel_id=1, source_target_pairs={{0,16},{16,0},{1,17},{17,1},{2,18},{18,2},{3,19},{19,3},{4,20},{20... | collective-permute-start | bytes 786440 | tf_op jit(solution)/shard_map/ppermute | solution.py:17
  114.8 29.6 %while.18 = (s32[]{:T(128)}, f32[2,128,256]{2,1,0:T(8,128)S(1)}, f32[2,128,256]{2,1,0:T(8,128)S(1)}, f32[256,16]{0,1:T(8,128)}, f32[256,16]{0,1:T(8,128)}, /*ind...) while((s32[]{:T(128)}, f32[2,128,256]{2,1,0:T(8,128)S(1)}, ...), condition=%wide.region_1.2_spmd.clone.clone.clone, body=%wide.region_0.1_spmd.clone.clone.clone.sunk | while | flops 921377 | bytes 1070735 | solution.py:160
  148.3 3.9 %collective-permute-start.2 = (bf16[2,2,128,1,256]{4,2,1,3,0:T(8,128)(2,1)}, bf16[2,2,128,1,256]{4,2,1,3,0:T(8,128)(2,1)S(1)}, u32[]{:S(2)}, u32[]{:S(2)}) collective-permute-start(bf16[2,2,128,1,256]{4,2,1,3,0:T(8,128)(2,1)} %get-tuple-element.293), channel_id=1, source_target_pairs={{0,8},{8,0},{1,9},{9,1},{2,10},{10,2},{3,11},{11,3},{4,12},{12,4},... | collective-permute-start | bytes 786440 | tf_op jit(solution)/shard_map/ppermute | solution.py:17
  156.6 8.9 %collective-permute-done.2 = bf16[2,2,128,1,256]{4,2,1,3,0:T(8,128)(2,1)S(1)} collective-permute-done((bf16[2,2,128,1,256]{4,2,1,3,0:T(8,128)(2,1)}, bf16[2,2,128,1,256]{4,2,1,3,0:T(8,128)(2,1)S(1)}, u32[]{:S(2)}, u32[]{:S(2)}) %collective-permute-start.2) | collective-permute-done | bytes 262176 | tf_op jit(solution)/shard_map/ppermute | solution.py:17
  167.7 6.3 %collective-permute-done.12 = bf16[2,2,128,1,256]{4,2,1,3,0:T(8,128)(2,1)S(1)} collective-permute-done((bf16[2,2,128,1,256]{4,2,1,3,0:T(8,128)(2,1)S(1)}, bf16[2,2,128,1,256]{4,2,1,3,0:T(8,128)(2,1)S(1)}, u32[]{:S(2)}, u32[]{:S(2)}) %collective-permute-start.12) | collective-permute-done | bytes 262176 | tf_op jit(solution)/shard_map/ppermute | solution.py:17
  176.1 3.2 collective-permute-done.3
  179.6 4.4 %collective-permute-start.4 = (bf16[2,2,128,1,256]{4,2,1,3,0:T(8,128)(2,1)S(1)}, bf16[2,2,128,1,256]{4,2,1,3,0:T(8,128)(2,1)S(1)}, u32[]{:S(2)}, u32[]{:S(2)}) collective-permute-start(bf16[2,2,128,1,256]{4,2,1,3,0:T(8,128)(2,1)S(1)} %get-tuple-element.289), channel_id=1, source_target_pairs={{0,2},{2,0},{1,3},{3,1},{4,6},{6,4},{5,7},{7,5},{8,10},{10,8},{9,1... | collective-permute-start | bytes 786440 | tf_op jit(solution)/shard_map/ppermute | solution.py:17
  185.2 4.7 %collective-permute-start.14 = (bf16[2,2,128,1,256]{4,2,1,3,0:T(8,128)(2,1)S(1)}, bf16[2,2,128,1,256]{4,2,1,3,0:T(8,128)(2,1)S(1)}, u32[]{:S(2)}, u32[]{:S(2)}) collective-permute-start(bf16[2,2,128,1,256]{4,2,1,3,0:T(8,128)(2,1)S(1)} %get-tuple-element.269), channel_id=1, source_target_pairs={{0,2},{2,0},{1,3},{3,1},{4,6},{6,4},{5,7},{7,5},{8,10},{10,8},{9,1... | collective-permute-start | bytes 786440 | tf_op jit(solution)/shard_map/ppermute | solution.py:17
  192.1 4.1 %collective-permute-done.14 = bf16[2,2,128,1,256]{4,2,1,3,0:T(8,128)(2,1)S(1)} collective-permute-done((bf16[2,2,128,1,256]{4,2,1,3,0:T(8,128)(2,1)S(1)}, bf16[2,2,128,1,256]{4,2,1,3,0:T(8,128)(2,1)S(1)}, u32[]{:S(2)}, u32[]{:S(2)}) %collective-permute-start.14) | collective-permute-done | bytes 262176 | tf_op jit(solution)/shard_map/ppermute | solution.py:17
  198.6 2.8 collective-permute-done.5
  203.1 3.9 %collective-permute-done.15 = bf16[2,2,128,1,256]{4,2,1,3,0:T(8,128)(2,1)S(1)} collective-permute-done((bf16[2,2,128,1,256]{4,2,1,3,0:T(8,128)(2,1)S(1)}, bf16[2,2,128,1,256]{4,2,1,3,0:T(8,128)(2,1)S(1)}, u32[]{:S(2)}, u32[]{:S(2)}) %collective-permute-start.15) | collective-permute-done | bytes 262176 | tf_op jit(solution)/shard_map/ppermute | solution.py:17
  217.1 3.5 collective-permute-start.6
  220.6 3.7 %collective-permute-done.6 = bf16[2,2,128,1,256]{4,2,1,3,0:T(8,128)(2,1)S(1)} collective-permute-done((bf16[2,2,128,1,256]{4,2,1,3,0:T(8,128)(2,1)S(1)}, bf16[2,2,128,1,256]{4,2,1,3,0:T(8,128)(2,1)S(1)}, u32[]{:S(2)}, u32[]{:S(2)}) %collective-permute-start.6) | collective-permute-done | bytes 262176 | tf_op jit(solution)/shard_map/ppermute | solution.py:17
  226.6 8.3 %collective-permute-done.7 = bf16[2,2,128,1,256]{4,2,1,3,0:T(8,128)(2,1)S(1)} collective-permute-done((bf16[2,2,128,1,256]{4,2,1,3,0:T(8,128)(2,1)S(1)}, bf16[2,2,128,1,256]{4,2,1,3,0:T(8,128)(2,1)S(1)}, u32[]{:S(2)}, u32[]{:S(2)}) %collective-permute-start.7) | collective-permute-done | bytes 262176 | tf_op jit(solution)/shard_map/ppermute | solution.py:17
  237.4 5.0 %collective-permute-done.8 = bf16[2,2,128,1,256]{4,2,1,3,0:T(8,128)(2,1)S(1)} collective-permute-done((bf16[2,2,128,1,256]{4,2,1,3,0:T(8,128)(2,1)S(1)}, bf16[2,2,128,1,256]{4,2,1,3,0:T(8,128)(2,1)S(1)}, u32[]{:S(2)}, u32[]{:S(2)}) %collective-permute-start.8) | collective-permute-done | bytes 262176 | tf_op jit(solution)/shard_map/ppermute | solution.py:17
  244.9 8.4 %collective-permute-done.9 = bf16[2,2,128,1,256]{4,2,1,3,0:T(8,128)(2,1)S(1)} collective-permute-done((bf16[2,2,128,1,256]{4,2,1,3,0:T(8,128)(2,1)S(1)}, bf16[2,2,128,1,256]{4,2,1,3,0:T(8,128)(2,1)S(1)}, u32[]{:S(2)}, u32[]{:S(2)}) %collective-permute-start.9) | collective-permute-done | bytes 262176 | tf_op jit(solution)/shard_map/ppermute | solution.py:17
  253.6 4.8 %collective-permute-start.10 = (bf16[2,2,128,1,256]{4,2,1,3,0:T(8,128)(2,1)S(1)}, bf16[2,2,128,1,256]{4,2,1,3,0:T(8,128)(2,1)S(1)}, u32[]{:S(2)}, u32[]{:S(2)}) collective-permute-start(bf16[2,2,128,1,256]{4,2,1,3,0:T(8,128)(2,1)S(1)} %get-tuple-element.275), channel_id=1, source_target_pairs={{0,16},{16,0},{1,17},{17,1},{2,18},{18,2},{3,19},{19,3},{4,20},{20... | collective-permute-start | bytes 786440 | tf_op jit(solution)/shard_map/ppermute | solution.py:17
  261.1 4.3 %collective-permute-done.10 = bf16[2,2,128,1,256]{4,2,1,3,0:T(8,128)(2,1)S(1)} collective-permute-done((bf16[2,2,128,1,256]{4,2,1,3,0:T(8,128)(2,1)S(1)}, bf16[2,2,128,1,256]{4,2,1,3,0:T(8,128)(2,1)S(1)}, u32[]{:S(2)}, u32[]{:S(2)}) %collective-permute-start.10) | collective-permute-done | bytes 262176 | tf_op jit(solution)/shard_map/ppermute | solution.py:17
  268.1 6.3 %collective-permute-start.17 = (bf16[2,2,128,1,256]{4,2,1,3,0:T(8,128)(2,1)S(1)}, bf16[2,2,128,1,256]{4,2,1,3,0:T(8,128)(2,1)S(1)}, u32[]{:S(2)}, u32[]{:S(2)}) collective-permute-start(bf16[2,2,128,1,256]{4,2,1,3,0:T(8,128)(2,1)S(1)} %get-tuple-element.261), channel_id=1, source_target_pairs={{0,2},{2,0},{1,3},{3,1},{4,6},{6,4},{5,7},{7,5},{8,10},{10,8},{9,1... | collective-permute-start | bytes 786440 | tf_op jit(solution)/shard_map/ppermute | solution.py:17
  274.4 4.0 %collective-permute-done.17 = bf16[2,2,128,1,256]{4,2,1,3,0:T(8,128)(2,1)S(1)} collective-permute-done((bf16[2,2,128,1,256]{4,2,1,3,0:T(8,128)(2,1)S(1)}, bf16[2,2,128,1,256]{4,2,1,3,0:T(8,128)(2,1)S(1)}, u32[]{:S(2)}, u32[]{:S(2)}) %collective-permute-start.17) | collective-permute-done | bytes 262176 | tf_op jit(solution)/shard_map/ppermute | solution.py:17
  278.6 3.2 collective-permute-start.18
  281.9 3.9 %collective-permute-done.18 = bf16[2,2,128,1,256]{4,2,1,3,0:T(8,128)(2,1)S(1)} collective-permute-done((bf16[2,2,128,1,256]{4,2,1,3,0:T(8,128)(2,1)S(1)}, bf16[2,2,128,1,256]{4,2,1,3,0:T(8,128)(2,1)S(1)}, u32[]{:S(2)}, u32[]{:S(2)}) %collective-permute-start.18) | collective-permute-done | bytes 262176 | tf_op jit(solution)/shard_map/ppermute | solution.py:17
  286.0 4.9 %collective-permute-start.19 = (bf16[2,2,128,1,256]{4,2,1,3,0:T(8,128)(2,1)S(1)}, bf16[2,2,128,1,256]{4,2,1,3,0:T(8,128)(2,1)S(1)}, u32[]{:S(2)}, u32[]{:S(2)}) collective-permute-start(bf16[2,2,128,1,256]{4,2,1,3,0:T(8,128)(2,1)S(1)} %get-tuple-element.257), channel_id=1, source_target_pairs={{0,8},{8,0},{1,9},{9,1},{2,10},{10,2},{3,11},{11,3},{4,12},{12,4},... | collective-permute-start | bytes 786440 | tf_op jit(solution)/shard_map/ppermute | solution.py:17
  290.9 6.6 %collective-permute-done.19 = bf16[2,2,128,1,256]{4,2,1,3,0:T(8,128)(2,1)S(1)} collective-permute-done((bf16[2,2,128,1,256]{4,2,1,3,0:T(8,128)(2,1)S(1)}, bf16[2,2,128,1,256]{4,2,1,3,0:T(8,128)(2,1)S(1)}, u32[]{:S(2)}, u32[]{:S(2)}) %collective-permute-start.19) | collective-permute-done | bytes 262176 | tf_op jit(solution)/shard_map/ppermute | solution.py:17
  297.8 5.7 %collective-permute-start.20 = (bf16[2,2,128,1,256]{4,2,1,3,0:T(8,128)(2,1)S(1)}, bf16[2,2,128,1,256]{4,2,1,3,0:T(8,128)(2,1)S(1)}, u32[]{:S(2)}, u32[]{:S(2)}) collective-permute-start(bf16[2,2,128,1,256]{4,2,1,3,0:T(8,128)(2,1)S(1)} %get-tuple-element.255), channel_id=1, source_target_pairs={{0,16},{16,0},{1,17},{17,1},{2,18},{18,2},{3,19},{19,3},{4,20},{20... | collective-permute-start | bytes 786440 | tf_op jit(solution)/shard_map/ppermute | solution.py:17
  303.5 7.9 %collective-permute-done.20 = bf16[2,2,128,1,256]{4,2,1,3,0:T(8,128)(2,1)S(1)} collective-permute-done((bf16[2,2,128,1,256]{4,2,1,3,0:T(8,128)(2,1)S(1)}, bf16[2,2,128,1,256]{4,2,1,3,0:T(8,128)(2,1)S(1)}, u32[]{:S(2)}, u32[]{:S(2)}) %collective-permute-start.20) | collective-permute-done | bytes 262176 | tf_op jit(solution)/shard_map/ppermute | solution.py:17
  313.1 3.5 collective-permute-done.21
  317.4 29.9 %reduce-scatter.2.cloned.1.call-done = bf16[128,512]{1,0:T(8,128)(2,1)} async-done(((bf16[128,8192]{1,0:T(8,128)(2,1)}), bf16[128,512]{1,0:T(8,128)(2,1)}) %reduce-scatter.2.cloned.1.call-update) | async-done | bytes 131088 | tf_op jit(solution)/shard_map/reduce_scatter | solution.py:195
  (231 shorter events, 79.4 us)
Async XLA Ops:
  7.2 98.9 %copy-start = (bf16[128,8192]{1,0:T(8,128)(2,1)S(1)}, bf16[128,8192]{1,0:T(8,128)(2,1)}, u32[]{:S(2)}) copy-start(bf16[128,8192]{1,0:T(8,128)(2,1)} %param.13) | copy-start | bytes 6291460
  7.2 98.9 %all-gather.2.cloned.1.call-start = ((), (), s32[]{:S(2)}) async-start(), calls=%async_computation.1 | async-start | bytes 4325376 | tf_op jit(solution)/shard_map/all_gather | solution.py:193
  7.9 339.4 %reduce-scatter.2.cloned.1.call-start = ((), (), s32[]{:S(2)}) async-start(), calls=%async_computation.2 | async-start | bytes 2228224 | tf_op jit(solution)/shard_map/reduce_scatter | solution.py:195
  8.7 5.6 %collective-permute-start = (bf16[2,3,256]{2,0,1:T(2,128)(2,1)S(1)}, bf16[2,3,256]{2,0,1:T(2,128)(2,1)S(1)}, u32[]{:S(2)}, u32[]{:S(2)}) collective-permute-start(bf16[2,3,256]{2,0,1:T(2,128)(2,1)S(1)} %slice.158), channel_id=1, source_target_pairs={{0,1},{1,2},{2,3},{3,4},{4,5},{5,6},{6,7},{7,8},{8,9},{9,10},{10,1... | collective-permute-start | bytes 9224 | tf_op jit(solution)/shard_map/ppermute | solution.py:23
  15.2 129.3 %collective-permute-start.1 = (bf16[2,2,128,1,256]{4,2,1,3,0:T(8,128)(2,1)}, bf16[2,2,128,1,256]{4,2,1,3,0:T(8,128)(2,1)}, u32[]{:S(2)}, u32[]{:S(2)}) collective-permute-start(bf16[2,2,128,1,256]{4,2,1,3,0:T(8,128)(2,1)} %fusion.53), channel_id=1, source_target_pairs={{0,16},{16,0},{1,17},{17,1},{2,18},{18,2},{3,19},{19,3},{4,20},{20... | collective-permute-start | bytes 786440 | tf_op jit(solution)/shard_map/ppermute | solution.py:17
  109.8 0.7 copy-start.3
  110.5 35.0 %collective-permute-start.11 = (bf16[2,2,128,1,256]{4,2,1,3,0:T(8,128)(2,1)S(1)}, bf16[2,2,128,1,256]{4,2,1,3,0:T(8,128)(2,1)S(1)}, u32[]{:S(2)}, u32[]{:S(2)}) collective-permute-start(bf16[2,2,128,1,256]{4,2,1,3,0:T(8,128)(2,1)S(1)} %fusion.52), channel_id=1, source_target_pairs={{0,16},{16,0},{1,17},{17,1},{2,18},{18,2},{3,19},{19,3},{4,20},{20... | collective-permute-start | bytes 786440 | tf_op jit(solution)/shard_map/ppermute | solution.py:17
  148.3 17.2 %collective-permute-start.2 = (bf16[2,2,128,1,256]{4,2,1,3,0:T(8,128)(2,1)}, bf16[2,2,128,1,256]{4,2,1,3,0:T(8,128)(2,1)S(1)}, u32[]{:S(2)}, u32[]{:S(2)}) collective-permute-start(bf16[2,2,128,1,256]{4,2,1,3,0:T(8,128)(2,1)} %get-tuple-element.293), channel_id=1, source_target_pairs={{0,8},{8,0},{1,9},{9,1},{2,10},{10,2},{3,11},{11,3},{4,12},{12,4},... | collective-permute-start | bytes 786440 | tf_op jit(solution)/shard_map/ppermute | solution.py:17
  154.3 19.7 %collective-permute-start.12 = (bf16[2,2,128,1,256]{4,2,1,3,0:T(8,128)(2,1)S(1)}, bf16[2,2,128,1,256]{4,2,1,3,0:T(8,128)(2,1)S(1)}, u32[]{:S(2)}, u32[]{:S(2)}) collective-permute-start(bf16[2,2,128,1,256]{4,2,1,3,0:T(8,128)(2,1)S(1)} %get-tuple-element.273), channel_id=1, source_target_pairs={{0,8},{8,0},{1,9},{9,1},{2,10},{10,2},{3,11},{11,3},{4,12},{12,4},... | collective-permute-start | bytes 786440 | tf_op jit(solution)/shard_map/ppermute | solution.py:17
  165.7 13.6 %collective-permute-start.3 = (bf16[2,2,128,1,256]{4,2,1,3,0:T(8,128)(2,1)S(1)}, bf16[2,2,128,1,256]{4,2,1,3,0:T(8,128)(2,1)S(1)}, u32[]{:S(2)}, u32[]{:S(2)}) collective-permute-start(bf16[2,2,128,1,256]{4,2,1,3,0:T(8,128)(2,1)S(1)} %get-tuple-element.291), channel_id=1, source_target_pairs={{0,4},{4,0},{1,5},{5,1},{2,6},{6,2},{3,7},{7,3},{8,12},{12,8},{9,1... | collective-permute-start | bytes 786440 | tf_op jit(solution)/shard_map/ppermute | solution.py:17
  174.2 10.8 %collective-permute-start.13 = (bf16[2,2,128,1,256]{4,2,1,3,0:T(8,128)(2,1)S(1)}, bf16[2,2,128,1,256]{4,2,1,3,0:T(8,128)(2,1)S(1)}, u32[]{:S(2)}, u32[]{:S(2)}) collective-permute-start(bf16[2,2,128,1,256]{4,2,1,3,0:T(8,128)(2,1)S(1)} %get-tuple-element.271), channel_id=1, source_target_pairs={{0,4},{4,0},{1,5},{5,1},{2,6},{6,2},{3,7},{7,3},{8,12},{12,8},{9,1... | collective-permute-start | bytes 786440 | tf_op jit(solution)/shard_map/ppermute | solution.py:17
  179.6 10.3 %collective-permute-start.4 = (bf16[2,2,128,1,256]{4,2,1,3,0:T(8,128)(2,1)S(1)}, bf16[2,2,128,1,256]{4,2,1,3,0:T(8,128)(2,1)S(1)}, u32[]{:S(2)}, u32[]{:S(2)}) collective-permute-start(bf16[2,2,128,1,256]{4,2,1,3,0:T(8,128)(2,1)S(1)} %get-tuple-element.289), channel_id=1, source_target_pairs={{0,2},{2,0},{1,3},{3,1},{4,6},{6,4},{5,7},{7,5},{8,10},{10,8},{9,1... | collective-permute-start | bytes 786440 | tf_op jit(solution)/shard_map/ppermute | solution.py:17
  185.2 11.0 %collective-permute-start.14 = (bf16[2,2,128,1,256]{4,2,1,3,0:T(8,128)(2,1)S(1)}, bf16[2,2,128,1,256]{4,2,1,3,0:T(8,128)(2,1)S(1)}, u32[]{:S(2)}, u32[]{:S(2)}) collective-permute-start(bf16[2,2,128,1,256]{4,2,1,3,0:T(8,128)(2,1)S(1)} %get-tuple-element.269), channel_id=1, source_target_pairs={{0,2},{2,0},{1,3},{3,1},{4,6},{6,4},{5,7},{7,5},{8,10},{10,8},{9,1... | collective-permute-start | bytes 786440 | tf_op jit(solution)/shard_map/ppermute | solution.py:17
  190.2 11.2 %collective-permute-start.5 = (bf16[2,2,128,1,256]{4,2,1,3,0:T(8,128)(2,1)S(1)}, bf16[2,2,128,1,256]{4,2,1,3,0:T(8,128)(2,1)S(1)}, u32[]{:S(2)}, u32[]{:S(2)}) collective-permute-start(bf16[2,2,128,1,256]{4,2,1,3,0:T(8,128)(2,1)S(1)} %get-tuple-element.287), channel_id=1, source_target_pairs={{0,1},{1,0},{2,3},{3,2},{4,5},{5,4},{6,7},{7,6},{8,9},{9,8},{10,11... | collective-permute-start | bytes 786440 | tf_op jit(solution)/shard_map/ppermute | solution.py:17
  196.5 10.5 %collective-permute-start.15 = (bf16[2,2,128,1,256]{4,2,1,3,0:T(8,128)(2,1)S(1)}, bf16[2,2,128,1,256]{4,2,1,3,0:T(8,128)(2,1)S(1)}, u32[]{:S(2)}, u32[]{:S(2)}) collective-permute-start(bf16[2,2,128,1,256]{4,2,1,3,0:T(8,128)(2,1)S(1)} %get-tuple-element.267), channel_id=1, source_target_pairs={{0,1},{1,0},{2,3},{3,2},{4,5},{5,4},{6,7},{7,6},{8,9},{9,8},{10,11... | collective-permute-start | bytes 786440 | tf_op jit(solution)/shard_map/ppermute | solution.py:17
  217.1 7.3 %collective-permute-start.6 = (bf16[2,2,128,1,256]{4,2,1,3,0:T(8,128)(2,1)S(1)}, bf16[2,2,128,1,256]{4,2,1,3,0:T(8,128)(2,1)S(1)}, u32[]{:S(2)}, u32[]{:S(2)}) collective-permute-start(bf16[2,2,128,1,256]{4,2,1,3,0:T(8,128)(2,1)S(1)} %pad_maximum_fusion.5), channel_id=1, source_target_pairs={{0,1},{1,0},{2,3},{3,2},{4,5},{5,4},{6,7},{7,6},{8,9},{9,8},{10,11... | collective-permute-start | bytes 786440 | tf_op jit(solution)/shard_map/ppermute | solution.py:17
  224.7 10.3 %collective-permute-start.7 = (bf16[2,2,128,1,256]{4,2,1,3,0:T(8,128)(2,1)S(1)}, bf16[2,2,128,1,256]{4,2,1,3,0:T(8,128)(2,1)S(1)}, u32[]{:S(2)}, u32[]{:S(2)}) collective-permute-start(bf16[2,2,128,1,256]{4,2,1,3,0:T(8,128)(2,1)S(1)} %get-tuple-element.281), channel_id=1, source_target_pairs={{0,2},{2,0},{1,3},{3,1},{4,6},{6,4},{5,7},{7,5},{8,10},{10,8},{9,1... | collective-permute-start | bytes 786440 | tf_op jit(solution)/shard_map/ppermute | solution.py:17
  235.2 7.1 %collective-permute-start.8 = (bf16[2,2,128,1,256]{4,2,1,3,0:T(8,128)(2,1)S(1)}, bf16[2,2,128,1,256]{4,2,1,3,0:T(8,128)(2,1)S(1)}, u32[]{:S(2)}, u32[]{:S(2)}) collective-permute-start(bf16[2,2,128,1,256]{4,2,1,3,0:T(8,128)(2,1)S(1)} %get-tuple-element.279), channel_id=1, source_target_pairs={{0,4},{4,0},{1,5},{5,1},{2,6},{6,2},{3,7},{7,3},{8,12},{12,8},{9,1... | collective-permute-start | bytes 786440 | tf_op jit(solution)/shard_map/ppermute | solution.py:17
  242.6 10.7 %collective-permute-start.9 = (bf16[2,2,128,1,256]{4,2,1,3,0:T(8,128)(2,1)S(1)}, bf16[2,2,128,1,256]{4,2,1,3,0:T(8,128)(2,1)S(1)}, u32[]{:S(2)}, u32[]{:S(2)}) collective-permute-start(bf16[2,2,128,1,256]{4,2,1,3,0:T(8,128)(2,1)S(1)} %get-tuple-element.277), channel_id=1, source_target_pairs={{0,8},{8,0},{1,9},{9,1},{2,10},{10,2},{3,11},{11,3},{4,12},{12,4},... | collective-permute-start | bytes 786440 | tf_op jit(solution)/shard_map/ppermute | solution.py:17
  253.4 12.3 %copy-start.4 = (f32[128,256]{1,0:T(8,128)S(1)}, f32[128,256]{1,0:T(8,128)}, u32[]{:S(2)}) copy-start(f32[128,256]{1,0:T(8,128)} %copy-done.3) | copy-start | bytes 393220
  253.5 12.2 %copy-start.2 = (bf16[256,8192]{1,0:T(8,128)(2,1)S(1)}, bf16[256,8192]{1,0:T(8,128)(2,1)}, u32[]{:S(2)}) copy-start(bf16[256,8192]{1,0:T(8,128)(2,1)} %all-gather.2.cloned.1.call-done) | copy-start | bytes 12582916
  253.6 11.8 %collective-permute-start.10 = (bf16[2,2,128,1,256]{4,2,1,3,0:T(8,128)(2,1)S(1)}, bf16[2,2,128,1,256]{4,2,1,3,0:T(8,128)(2,1)S(1)}, u32[]{:S(2)}, u32[]{:S(2)}) collective-permute-start(bf16[2,2,128,1,256]{4,2,1,3,0:T(8,128)(2,1)S(1)} %get-tuple-element.275), channel_id=1, source_target_pairs={{0,16},{16,0},{1,17},{17,1},{2,18},{18,2},{3,19},{19,3},{4,20},{20... | collective-permute-start | bytes 786440 | tf_op jit(solution)/shard_map/ppermute | solution.py:17
  258.5 9.4 %collective-permute-start.16 = (bf16[2,2,128,1,256]{4,2,1,3,0:T(8,128)(2,1)S(1)}, bf16[2,2,128,1,256]{4,2,1,3,0:T(8,128)(2,1)S(1)}, u32[]{:S(2)}, u32[]{:S(2)}) collective-permute-start(bf16[2,2,128,1,256]{4,2,1,3,0:T(8,128)(2,1)S(1)} %pad_maximum_fusion.6), channel_id=1, source_target_pairs={{0,1},{1,0},{2,3},{3,2},{4,5},{5,4},{6,7},{7,6},{8,9},{9,8},{10,11... | collective-permute-start | bytes 786440 | tf_op jit(solution)/shard_map/ppermute | solution.py:17
  268.1 10.2 %collective-permute-start.17 = (bf16[2,2,128,1,256]{4,2,1,3,0:T(8,128)(2,1)S(1)}, bf16[2,2,128,1,256]{4,2,1,3,0:T(8,128)(2,1)S(1)}, u32[]{:S(2)}, u32[]{:S(2)}) collective-permute-start(bf16[2,2,128,1,256]{4,2,1,3,0:T(8,128)(2,1)S(1)} %get-tuple-element.261), channel_id=1, source_target_pairs={{0,2},{2,0},{1,3},{3,1},{4,6},{6,4},{5,7},{7,5},{8,10},{10,8},{9,1... | collective-permute-start | bytes 786440 | tf_op jit(solution)/shard_map/ppermute | solution.py:17
  278.6 7.1 %collective-permute-start.18 = (bf16[2,2,128,1,256]{4,2,1,3,0:T(8,128)(2,1)S(1)}, bf16[2,2,128,1,256]{4,2,1,3,0:T(8,128)(2,1)S(1)}, u32[]{:S(2)}, u32[]{:S(2)}) collective-permute-start(bf16[2,2,128,1,256]{4,2,1,3,0:T(8,128)(2,1)S(1)} %get-tuple-element.259), channel_id=1, source_target_pairs={{0,4},{4,0},{1,5},{5,1},{2,6},{6,2},{3,7},{7,3},{8,12},{12,8},{9,1... | collective-permute-start | bytes 786440 | tf_op jit(solution)/shard_map/ppermute | solution.py:17
  286.0 11.4 %collective-permute-start.19 = (bf16[2,2,128,1,256]{4,2,1,3,0:T(8,128)(2,1)S(1)}, bf16[2,2,128,1,256]{4,2,1,3,0:T(8,128)(2,1)S(1)}, u32[]{:S(2)}, u32[]{:S(2)}) collective-permute-start(bf16[2,2,128,1,256]{4,2,1,3,0:T(8,128)(2,1)S(1)} %get-tuple-element.257), channel_id=1, source_target_pairs={{0,8},{8,0},{1,9},{9,1},{2,10},{10,2},{3,11},{11,3},{4,12},{12,4},... | collective-permute-start | bytes 786440 | tf_op jit(solution)/shard_map/ppermute | solution.py:17
  297.8 49.5 %copy-start.1 = (bf16[128,8192]{1,0:T(8,128)(2,1)S(1)}, bf16[128,8192]{1,0:T(8,128)(2,1)}, u32[]{:S(2)}) copy-start(bf16[128,8192]{1,0:T(8,128)(2,1)} %param.13) | copy-start | bytes 6291460
  297.8 13.6 %collective-permute-start.20 = (bf16[2,2,128,1,256]{4,2,1,3,0:T(8,128)(2,1)S(1)}, bf16[2,2,128,1,256]{4,2,1,3,0:T(8,128)(2,1)S(1)}, u32[]{:S(2)}, u32[]{:S(2)}) collective-permute-start(bf16[2,2,128,1,256]{4,2,1,3,0:T(8,128)(2,1)S(1)} %get-tuple-element.255), channel_id=1, source_target_pairs={{0,16},{16,0},{1,17},{17,1},{2,18},{18,2},{3,19},{19,3},{4,20},{20... | collective-permute-start | bytes 786440 | tf_op jit(solution)/shard_map/ppermute | solution.py:17
  311.8 4.8 %collective-permute-start.21 = (f32[2,3,256]{2,0,1:T(2,128)S(1)}, f32[2,3,256]{2,0,1:T(2,128)S(1)}, u32[]{:S(2)}, u32[]{:S(2)}) collective-permute-start(f32[2,3,256]{2,0,1:T(2,128)S(1)} %slice.482), channel_id=1, source_target_pairs={{1,0},{2,1},{3,2},{4,3},{5,4},{6,5},{7,6},{8,7},{9,8},{10,9},{11,1... | collective-permute-start | bytes 18440 | tf_op jit(solution)/shard_map/ppermute | solution.py:23
Sparse Core Ops, SparseCore 0:
  11.0 95.0 all-gather.1
  267.9 79.3 reduce-scatter.1
where the time goes:
time: 357 us; the launch traced here: 354 us
  waiting for transfers between devices  195 us (55%)
  starting transfers between devices  81.9 us (23%)
  other arithmetic  41.7 us (12%)
  matrix products  17 us (5%)
  between operations  15.9 us (4%)
    ppermute x20, waiting for transfers between devices, swapped(): return lax.ppermute(block, axis, route)  82.4 us
    all_gather x1, waiting for transfers between devices, per_device(): w_full = lax.all_gather(w_out, 'ctx', axis=1, tiled=True)  78.2 us
    ppermute x20, starting transfers between devices, swapped(): return lax.ppermute(block, axis, route)  77.5 us
    reduce_scatter x1, waiting for transfers between devices, per_device(): lax.psum_scatter(partial_sum.astype(jnp.bfloat16), 'fsdp', scatter_dimens...  29.9 us
    mul x16, other arithmetic, add_mode(): denom_im = decay_now * full_sine  12.1 us
    mul x16, other arithmetic, add_mode(): lax.dynamic_slice_in_dim(residues, mode_index, 1, 1)[:, 0]  11.8 us
  transfers between devices with their start and end apart: 24, of which 19 were waited for; matrix products, arithmetic and copies ran while one was open for 13% of the time, Pallas kernels for 0%

commit v1 on v0

--- a/solution.py
+++ b/solution.py
@@ -190,7 +190,9 @@
     conv_im = signal_re * filter_im + signal_im * filter_re
     convolved = from_spectrum(conv_re, conv_im)[:, 0]
     gated_out = (query_part * convolved).astype(jnp.bfloat16)
-    w_full = lax.all_gather(w_out, "ctx", axis=1, tiled=True)
+    w_full = jnp.concatenate(
+        lax.all_to_all(jnp.stack([w_out] * lax.axis_size("ctx")), "ctx", 0, 0), axis=1
+    )
     partial_sum = jnp.dot(gated_out, w_full, preferred_element_type=jnp.float32)
     block_output = lax.psum_scatter(
         partial_sum.astype(jnp.bfloat16), "fsdp", scatter_dimension=1, tiled=True

time: 357 us -> 370 us (1.036)
  the two profiles are of different devices: /device:TPU:25 before, /device:TPU:27 now
where the time goes in v1:
time: 370 us; the launch traced here: 367 us
  waiting for transfers between devices  180 us (49%)
  starting transfers between devices  105 us (28%)
  other arithmetic  41.6 us (11%)
  matrix products  19.2 us (5%)
  between operations  15.9 us (4%)
  local copies, waits for them, and re-layouts  4.57 us (1%)
    ppermute x20, starting transfers between devices, swapped(): return lax.ppermute(block, axis, route)  86.4 us
    all_to_all x1, waiting for transfers between devices, per_device(): lax.all_to_all(jnp.stack([w_out] * lax.axis_size('ctx')), 'ctx', 0, 0)  73.7 us
    ppermute x20, waiting for transfers between devices, swapped(): return lax.ppermute(block, axis, route)  72.9 us
    reduce_scatter x1, waiting for transfers between devices, per_device(): lax.psum_scatter(partial_sum.astype(jnp.bfloat16), 'fsdp', scatter_dimens...  24 us
    all_to_all x1, starting transfers between devices, per_device(): lax.all_to_all(jnp.stack([w_out] * lax.axis_size('ctx')), 'ctx', 0, 0)  13.1 us
    mul x16, other arithmetic, add_mode(): denom_im = decay_now * full_sine  12.8 us
    mul x16, other arithmetic, add_mode(): lax.dynamic_slice_in_dim(residues, mode_index, 1, 1)[:, 0]  11.8 us
    ppermute x2, waiting for transfers between devices, shifted(): return lax.ppermute(block, axis, route)  9.54 us
  transfers between devices with their start and end apart: 24, of which 21 were waited for; matrix products, arithmetic and copies ran while one was open for 13% of the time, Pallas kernels for 0%

profile of v1, /device:TPU:27, one launch (start us, length us, event | category | flops | bytes accessed | tf_op | source)
XLA Modules:
  0.0 367.4 jit_solution(3908873842958064139)
XLA Ops:
  10.9 13.1 %all-to-all-start = ((bf16[32,256,256]{1,2,0:T(8,128)(2,1)}), bf16[32,256,256]{1,2,0:T(8,128)(2,1)}, u32[]{:S(2)}, u32[]{:S(2)}) async-start(bf16[32,256,256]{1,2,0:T(8,128)(2,1)} %stack.298), calls=%async_computation | async-start | bytes 8388608 | tf_op jit(solution)/shard_map/all_to_all | solution.py:194
  24.0 3.1 collective-permute-start
  28.0 5.8 %collective-permute-done = bf16[2,3,256]{2,0,1:T(2,128)(2,1)S(1)} collective-permute-done((bf16[2,3,256]{2,0,1:T(2,128)(2,1)S(1)}, bf16[2,3,256]{2,0,1:T(2,128)(2,1)S(1)}, u32[]{:S(2)}, u32[]{:S(2)}) %collective-permute-start) | collective-permute-done | bytes 3104 | tf_op jit(solution)/shard_map/ppermute | solution.py:23
  34.7 9.9 %collective-permute-start.1 = (bf16[2,2,128,1,256]{4,2,1,3,0:T(8,128)(2,1)}, bf16[2,2,128,1,256]{4,2,1,3,0:T(8,128)(2,1)}, u32[]{:S(2)}, u32[]{:S(2)}) collective-permute-start(bf16[2,2,128,1,256]{4,2,1,3,0:T(8,128)(2,1)} %fusion.53), channel_id=1, source_target_pairs={{0,16},{16,0},{1,17},{17,1},{2,18},{18,2},{3,19},{19,3},{4,20},{20... | collective-permute-start | bytes 786440 | tf_op jit(solution)/shard_map/ppermute | solution.py:17
  44.7 73.7 %all-to-all-done = bf16[32,256,256]{1,2,0:T(8,128)(2,1)} async-done(((bf16[32,256,256]{1,2,0:T(8,128)(2,1)}), bf16[32,256,256]{1,2,0:T(8,128)(2,1)}, u32[]{:S(2)}, u32[]{:S(2)}) %all-to-all-start) | async-done | bytes 4194336 | tf_op jit(solution)/shard_map/all_to_all | solution.py:194
  124.0 30.3 %while.18 = (s32[]{:T(128)}, f32[2,128,256]{2,1,0:T(8,128)S(1)}, f32[2,128,256]{2,1,0:T(8,128)S(1)}, f32[256,16]{0,1:T(8,128)}, f32[256,16]{0,1:T(8,128)}, /*ind...) while((s32[]{:T(128)}, f32[2,128,256]{2,1,0:T(8,128)S(1)}, ...), condition=%wide.region_1.2_spmd.clone.clone.clone, body=%wide.region_0.1_spmd.clone.clone.clone.sunk | while | flops 921377 | bytes 1070735 | solution.py:160
  158.3 10.6 %collective-permute-start.2 = (bf16[2,2,128,1,256]{4,2,1,3,0:T(8,128)(2,1)}, bf16[2,2,128,1,256]{4,2,1,3,0:T(8,128)(2,1)S(1)}, u32[]{:S(2)}, u32[]{:S(2)}) collective-permute-start(bf16[2,2,128,1,256]{4,2,1,3,0:T(8,128)(2,1)} %get-tuple-element.293), channel_id=1, source_target_pairs={{0,8},{8,0},{1,9},{9,1},{2,10},{10,2},{3,11},{11,3},{4,12},{12,4},... | collective-permute-start | bytes 786440 | tf_op jit(solution)/shard_map/ppermute | solution.py:17
  172.8 9.3 %collective-permute-done.2 = bf16[2,2,128,1,256]{4,2,1,3,0:T(8,128)(2,1)S(1)} collective-permute-done((bf16[2,2,128,1,256]{4,2,1,3,0:T(8,128)(2,1)}, bf16[2,2,128,1,256]{4,2,1,3,0:T(8,128)(2,1)S(1)}, u32[]{:S(2)}, u32[]{:S(2)}) %collective-permute-start.2) | collective-permute-done | bytes 262176 | tf_op jit(solution)/shard_map/ppermute | solution.py:17
  184.3 3.5 collective-permute-done.12
  189.9 2.9 collective-permute-done.3
  202.6 4.6 %collective-permute-start.5 = (bf16[2,2,128,1,256]{4,2,1,3,0:T(8,128)(2,1)S(1)}, bf16[2,2,128,1,256]{4,2,1,3,0:T(8,128)(2,1)S(1)}, u32[]{:S(2)}, u32[]{:S(2)}) collective-permute-start(bf16[2,2,128,1,256]{4,2,1,3,0:T(8,128)(2,1)S(1)} %get-tuple-element.287), channel_id=1, source_target_pairs={{0,1},{1,0},{2,3},{3,2},{4,5},{5,4},{6,7},{7,6},{8,9},{9,8},{10,11... | collective-permute-start | bytes 786440 | tf_op jit(solution)/shard_map/ppermute | solution.py:17
  209.0 4.5 %collective-permute-start.15 = (bf16[2,2,128,1,256]{4,2,1,3,0:T(8,128)(2,1)S(1)}, bf16[2,2,128,1,256]{4,2,1,3,0:T(8,128)(2,1)S(1)}, u32[]{:S(2)}, u32[]{:S(2)}) collective-permute-start(bf16[2,2,128,1,256]{4,2,1,3,0:T(8,128)(2,1)S(1)} %get-tuple-element.267), channel_id=1, source_target_pairs={{0,1},{1,0},{2,3},{3,2},{4,5},{5,4},{6,7},{7,6},{8,9},{9,8},{10,11... | collective-permute-start | bytes 786440 | tf_op jit(solution)/shard_map/ppermute | solution.py:17
  231.4 5.2 %collective-permute-done.6 = bf16[2,2,128,1,256]{4,2,1,3,0:T(8,128)(2,1)S(1)} collective-permute-done((bf16[2,2,128,1,256]{4,2,1,3,0:T(8,128)(2,1)S(1)}, bf16[2,2,128,1,256]{4,2,1,3,0:T(8,128)(2,1)S(1)}, u32[]{:S(2)}, u32[]{:S(2)}) %collective-permute-start.6) | collective-permute-done | bytes 262176 | tf_op jit(solution)/shard_map/ppermute | solution.py:17
  236.9 4.3 %collective-permute-start.7 = (bf16[2,2,128,1,256]{4,2,1,3,0:T(8,128)(2,1)S(1)}, bf16[2,2,128,1,256]{4,2,1,3,0:T(8,128)(2,1)S(1)}, u32[]{:S(2)}, u32[]{:S(2)}) collective-permute-start(bf16[2,2,128,1,256]{4,2,1,3,0:T(8,128)(2,1)S(1)} %get-tuple-element.281), channel_id=1, source_target_pairs={{0,2},{2,0},{1,3},{3,1},{4,6},{6,4},{5,7},{7,5},{8,10},{10,8},{9,1... | collective-permute-start | bytes 786440 | tf_op jit(solution)/shard_map/ppermute | solution.py:17
  241.2 4.9 %collective-permute-done.7 = bf16[2,2,128,1,256]{4,2,1,3,0:T(8,128)(2,1)S(1)} collective-permute-done((bf16[2,2,128,1,256]{4,2,1,3,0:T(8,128)(2,1)S(1)}, bf16[2,2,128,1,256]{4,2,1,3,0:T(8,128)(2,1)S(1)}, u32[]{:S(2)}, u32[]{:S(2)}) %collective-permute-start.7) | collective-permute-done | bytes 262176 | tf_op jit(solution)/shard_map/ppermute | solution.py:17
  246.4 3.3 collective-permute-start.8
  249.7 4.1 %collective-permute-done.8 = bf16[2,2,128,1,256]{4,2,1,3,0:T(8,128)(2,1)S(1)} collective-permute-done((bf16[2,2,128,1,256]{4,2,1,3,0:T(8,128)(2,1)S(1)}, bf16[2,2,128,1,256]{4,2,1,3,0:T(8,128)(2,1)S(1)}, u32[]{:S(2)}, u32[]{:S(2)}) %collective-permute-start.8) | collective-permute-done | bytes 262176 | tf_op jit(solution)/shard_map/ppermute | solution.py:17
  254.1 4.9 %collective-permute-start.9 = (bf16[2,2,128,1,256]{4,2,1,3,0:T(8,128)(2,1)S(1)}, bf16[2,2,128,1,256]{4,2,1,3,0:T(8,128)(2,1)S(1)}, u32[]{:S(2)}, u32[]{:S(2)}) collective-permute-start(bf16[2,2,128,1,256]{4,2,1,3,0:T(8,128)(2,1)S(1)} %get-tuple-element.277), channel_id=1, source_target_pairs={{0,8},{8,0},{1,9},{9,1},{2,10},{10,2},{3,11},{11,3},{4,12},{12,4},... | collective-permute-start | bytes 786440 | tf_op jit(solution)/shard_map/ppermute | solution.py:17
  259.0 6.6 %collective-permute-done.9 = bf16[2,2,128,1,256]{4,2,1,3,0:T(8,128)(2,1)S(1)} collective-permute-done((bf16[2,2,128,1,256]{4,2,1,3,0:T(8,128)(2,1)S(1)}, bf16[2,2,128,1,256]{4,2,1,3,0:T(8,128)(2,1)S(1)}, u32[]{:S(2)}, u32[]{:S(2)}) %collective-permute-start.9) | collective-permute-done | bytes 262176 | tf_op jit(solution)/shard_map/ppermute | solution.py:17
  265.9 6.2 %collective-permute-start.10 = (bf16[2,2,128,1,256]{4,2,1,3,0:T(8,128)(2,1)S(1)}, bf16[2,2,128,1,256]{4,2,1,3,0:T(8,128)(2,1)S(1)}, u32[]{:S(2)}, u32[]{:S(2)}) collective-permute-start(bf16[2,2,128,1,256]{4,2,1,3,0:T(8,128)(2,1)S(1)} %get-tuple-element.275), channel_id=1, source_target_pairs={{0,16},{16,0},{1,17},{17,1},{2,18},{18,2},{3,19},{19,3},{4,20},{20... | collective-permute-start | bytes 786440 | tf_op jit(solution)/shard_map/ppermute | solution.py:17
  274.2 3.5 collective-permute-done.10
  278.0 5.0 %convolution_convert_fusion = bf16[128,8192]{1,0:T(8,128)(2,1)} fusion(bf16[256,8192]{0,1:T(8,128)(2,1)} %bitcast.38, f32[1,1,128,1,256]{4,2,1,3,0:T(8,128)S(1)} %get-tuple-element.252, f32[128,3,256]{2,0,1:T(8,128)S(1)} %fusion.47), kind=kOutput, calls=%fused_computation.28 | convolution fusion | flops 537985024 | bytes 6553600 | tf_op jit(solution)/shard_map/dot_general | solution.py:196
  283.3 5.0 %collective-permute-start.17 = (bf16[2,2,128,1,256]{4,2,1,3,0:T(8,128)(2,1)S(1)}, bf16[2,2,128,1,256]{4,2,1,3,0:T(8,128)(2,1)S(1)}, u32[]{:S(2)}, u32[]{:S(2)}) collective-permute-start(bf16[2,2,128,1,256]{4,2,1,3,0:T(8,128)(2,1)S(1)} %get-tuple-element.261), channel_id=1, source_target_pairs={{0,2},{2,0},{1,3},{3,1},{4,6},{6,4},{5,7},{7,5},{8,10},{10,8},{9,1... | collective-permute-start | bytes 786440 | tf_op jit(solution)/shard_map/ppermute | solution.py:17
  288.3 5.8 %collective-permute-done.17 = bf16[2,2,128,1,256]{4,2,1,3,0:T(8,128)(2,1)S(1)} collective-permute-done((bf16[2,2,128,1,256]{4,2,1,3,0:T(8,128)(2,1)S(1)}, bf16[2,2,128,1,256]{4,2,1,3,0:T(8,128)(2,1)S(1)}, u32[]{:S(2)}, u32[]{:S(2)}) %collective-permute-start.17) | collective-permute-done | bytes 262176 | tf_op jit(solution)/shard_map/ppermute | solution.py:17
  294.4 4.0 %collective-permute-start.18 = (bf16[2,2,128,1,256]{4,2,1,3,0:T(8,128)(2,1)S(1)}, bf16[2,2,128,1,256]{4,2,1,3,0:T(8,128)(2,1)S(1)}, u32[]{:S(2)}, u32[]{:S(2)}) collective-permute-start(bf16[2,2,128,1,256]{4,2,1,3,0:T(8,128)(2,1)S(1)} %get-tuple-element.259), channel_id=1, source_target_pairs={{0,4},{4,0},{1,5},{5,1},{2,6},{6,2},{3,7},{7,3},{8,12},{12,8},{9,1... | collective-permute-start | bytes 786440 | tf_op jit(solution)/shard_map/ppermute | solution.py:17
  298.4 3.7 %collective-permute-done.18 = bf16[2,2,128,1,256]{4,2,1,3,0:T(8,128)(2,1)S(1)} collective-permute-done((bf16[2,2,128,1,256]{4,2,1,3,0:T(8,128)(2,1)S(1)}, bf16[2,2,128,1,256]{4,2,1,3,0:T(8,128)(2,1)S(1)}, u32[]{:S(2)}, u32[]{:S(2)}) %collective-permute-start.18) | collective-permute-done | bytes 262176 | tf_op jit(solution)/shard_map/ppermute | solution.py:17
  302.5 4.6 %collective-permute-start.19 = (bf16[2,2,128,1,256]{4,2,1,3,0:T(8,128)(2,1)S(1)}, bf16[2,2,128,1,256]{4,2,1,3,0:T(8,128)(2,1)S(1)}, u32[]{:S(2)}, u32[]{:S(2)}) collective-permute-start(bf16[2,2,128,1,256]{4,2,1,3,0:T(8,128)(2,1)S(1)} %get-tuple-element.257), channel_id=1, source_target_pairs={{0,8},{8,0},{1,9},{9,1},{2,10},{10,2},{3,11},{11,3},{4,12},{12,4},... | collective-permute-start | bytes 786440 | tf_op jit(solution)/shard_map/ppermute | solution.py:17
  307.1 6.6 %collective-permute-done.19 = bf16[2,2,128,1,256]{4,2,1,3,0:T(8,128)(2,1)S(1)} collective-permute-done((bf16[2,2,128,1,256]{4,2,1,3,0:T(8,128)(2,1)S(1)}, bf16[2,2,128,1,256]{4,2,1,3,0:T(8,128)(2,1)S(1)}, u32[]{:S(2)}, u32[]{:S(2)}) %collective-permute-start.19) | collective-permute-done | bytes 262176 | tf_op jit(solution)/shard_map/ppermute | solution.py:17
  313.9 6.9 %collective-permute-start.20 = (bf16[2,2,128,1,256]{4,2,1,3,0:T(8,128)(2,1)S(1)}, bf16[2,2,128,1,256]{4,2,1,3,0:T(8,128)(2,1)S(1)}, u32[]{:S(2)}, u32[]{:S(2)}) collective-permute-start(bf16[2,2,128,1,256]{4,2,1,3,0:T(8,128)(2,1)S(1)} %get-tuple-element.255), channel_id=1, source_target_pairs={{0,16},{16,0},{1,17},{17,1},{2,18},{18,2},{3,19},{19,3},{4,20},{20... | collective-permute-start | bytes 786440 | tf_op jit(solution)/shard_map/ppermute | solution.py:17
  320.9 8.0 %collective-permute-done.20 = bf16[2,2,128,1,256]{4,2,1,3,0:T(8,128)(2,1)S(1)} collective-permute-done((bf16[2,2,128,1,256]{4,2,1,3,0:T(8,128)(2,1)S(1)}, bf16[2,2,128,1,256]{4,2,1,3,0:T(8,128)(2,1)S(1)}, u32[]{:S(2)}, u32[]{:S(2)}) %collective-permute-start.20) | collective-permute-done | bytes 262176 | tf_op jit(solution)/shard_map/ppermute | solution.py:17
  332.0 3.8 %collective-permute-done.21 = f32[2,3,256]{2,0,1:T(2,128)S(1)} collective-permute-done((f32[2,3,256]{2,0,1:T(2,128)S(1)}, f32[2,3,256]{2,0,1:T(2,128)S(1)}, u32[]{:S(2)}, u32[]{:S(2)}) %collective-permute-start.21) | collective-permute-done | bytes 6176 | tf_op jit(solution)/shard_map/ppermute | solution.py:23
  336.6 24.0 %reduce-scatter.2.cloned.1.call-done = bf16[128,512]{1,0:T(8,128)(2,1)} async-done(((bf16[128,8192]{1,0:T(8,128)(2,1)}), bf16[128,512]{1,0:T(8,128)(2,1)}) %reduce-scatter.2.cloned.1.call-update) | async-done | bytes 131088 | tf_op jit(solution)/shard_map/reduce_scatter | solution.py:197
  (234 shorter events, 89.7 us)
Async XLA Ops:
  7.2 111.2 %copy-start = (bf16[128,8192]{1,0:T(8,128)(2,1)S(1)}, bf16[128,8192]{1,0:T(8,128)(2,1)}, u32[]{:S(2)}) copy-start(bf16[128,8192]{1,0:T(8,128)(2,1)} %param.13) | copy-start | bytes 6291460
  10.8 13.2 %copy-start.4 = (bf16[128,3,256]{2,0,1:T(8,128)(2,1)S(1)}, bf16[128,3,256]{2,0,1:T(8,128)(2,1)}, u32[]{:S(2)}) copy-start(bf16[128,3,256]{2,0,1:T(8,128)(2,1)} %param.8) | copy-start | bytes 589828
  10.8 16.9 %copy-start.5 = (f32[3,3,256]{2,1,0:T(4,128)S(1)}, f32[3,3,256]{2,1,0:T(4,128)}, u32[]{:S(2)}) copy-start(f32[3,3,256]{2,1,0:T(4,128)} %param.9) | copy-start | bytes 27652
  10.9 107.6 %all-to-all-start = ((bf16[32,256,256]{1,2,0:T(8,128)(2,1)}), bf16[32,256,256]{1,2,0:T(8,128)(2,1)}, u32[]{:S(2)}, u32[]{:S(2)}) async-start(bf16[32,256,256]{1,2,0:T(8,128)(2,1)} %stack.298), calls=%async_computation | async-start | bytes 8388608 | tf_op jit(solution)/shard_map/all_to_all | solution.py:194
  23.9 336.6 %reduce-scatter.2.cloned.1.call-start = ((), (), s32[]{:S(2)}) async-start(), calls=%async_computation.2 | async-start | bytes 2228224 | tf_op jit(solution)/shard_map/reduce_scatter | solution.py:197
  24.0 9.7 %collective-permute-start = (bf16[2,3,256]{2,0,1:T(2,128)(2,1)S(1)}, bf16[2,3,256]{2,0,1:T(2,128)(2,1)S(1)}, u32[]{:S(2)}, u32[]{:S(2)}) collective-permute-start(bf16[2,3,256]{2,0,1:T(2,128)(2,1)S(1)} %slice.158), channel_id=1, source_target_pairs={{0,1},{1,2},{2,3},{3,4},{4,5},{5,6},{6,7},{7,8},{8,9},{9,10},{10,1... | collective-permute-start | bytes 9224 | tf_op jit(solution)/shard_map/ppermute | solution.py:23
  34.7 119.7 %collective-permute-start.1 = (bf16[2,2,128,1,256]{4,2,1,3,0:T(8,128)(2,1)}, bf16[2,2,128,1,256]{4,2,1,3,0:T(8,128)(2,1)}, u32[]{:S(2)}, u32[]{:S(2)}) collective-permute-start(bf16[2,2,128,1,256]{4,2,1,3,0:T(8,128)(2,1)} %fusion.53), channel_id=1, source_target_pairs={{0,16},{16,0},{1,17},{17,1},{2,18},{18,2},{3,19},{19,3},{4,20},{20... | collective-permute-start | bytes 786440 | tf_op jit(solution)/shard_map/ppermute | solution.py:17
  121.3 0.7 copy-start.2
  122.0 33.4 %collective-permute-start.11 = (bf16[2,2,128,1,256]{4,2,1,3,0:T(8,128)(2,1)S(1)}, bf16[2,2,128,1,256]{4,2,1,3,0:T(8,128)(2,1)S(1)}, u32[]{:S(2)}, u32[]{:S(2)}) collective-permute-start(bf16[2,2,128,1,256]{4,2,1,3,0:T(8,128)(2,1)S(1)} %fusion.52), channel_id=1, source_target_pairs={{0,16},{16,0},{1,17},{17,1},{2,18},{18,2},{3,19},{19,3},{4,20},{20... | collective-permute-start | bytes 786440 | tf_op jit(solution)/shard_map/ppermute | solution.py:17
  158.3 23.8 %collective-permute-start.2 = (bf16[2,2,128,1,256]{4,2,1,3,0:T(8,128)(2,1)}, bf16[2,2,128,1,256]{4,2,1,3,0:T(8,128)(2,1)S(1)}, u32[]{:S(2)}, u32[]{:S(2)}) collective-permute-start(bf16[2,2,128,1,256]{4,2,1,3,0:T(8,128)(2,1)} %get-tuple-element.293), channel_id=1, source_target_pairs={{0,8},{8,0},{1,9},{9,1},{2,10},{10,2},{3,11},{11,3},{4,12},{12,4},... | collective-permute-start | bytes 786440 | tf_op jit(solution)/shard_map/ppermute | solution.py:17
  170.9 16.8 %collective-permute-start.12 = (bf16[2,2,128,1,256]{4,2,1,3,0:T(8,128)(2,1)S(1)}, bf16[2,2,128,1,256]{4,2,1,3,0:T(8,128)(2,1)S(1)}, u32[]{:S(2)}, u32[]{:S(2)}) collective-permute-start(bf16[2,2,128,1,256]{4,2,1,3,0:T(8,128)(2,1)S(1)} %get-tuple-element.273), channel_id=1, source_target_pairs={{0,8},{8,0},{1,9},{9,1},{2,10},{10,2},{3,11},{11,3},{4,12},{12,4},... | collective-permute-start | bytes 786440 | tf_op jit(solution)/shard_map/ppermute | solution.py:17
  182.3 10.5 %collective-permute-start.3 = (bf16[2,2,128,1,256]{4,2,1,3,0:T(8,128)(2,1)S(1)}, bf16[2,2,128,1,256]{4,2,1,3,0:T(8,128)(2,1)S(1)}, u32[]{:S(2)}, u32[]{:S(2)}) collective-permute-start(bf16[2,2,128,1,256]{4,2,1,3,0:T(8,128)(2,1)S(1)} %get-tuple-element.291), channel_id=1, source_target_pairs={{0,4},{4,0},{1,5},{5,1},{2,6},{6,2},{3,7},{7,3},{8,12},{12,8},{9,1... | collective-permute-start | bytes 786440 | tf_op jit(solution)/shard_map/ppermute | solution.py:17
  188.0 10.5 %collective-permute-start.13 = (bf16[2,2,128,1,256]{4,2,1,3,0:T(8,128)(2,1)S(1)}, bf16[2,2,128,1,256]{4,2,1,3,0:T(8,128)(2,1)S(1)}, u32[]{:S(2)}, u32[]{:S(2)}) collective-permute-start(bf16[2,2,128,1,256]{4,2,1,3,0:T(8,128)(2,1)S(1)} %get-tuple-element.271), channel_id=1, source_target_pairs={{0,4},{4,0},{1,5},{5,1},{2,6},{6,2},{3,7},{7,3},{8,12},{12,8},{9,1... | collective-permute-start | bytes 786440 | tf_op jit(solution)/shard_map/ppermute | solution.py:17
  193.0 9.3 %collective-permute-start.4 = (bf16[2,2,128,1,256]{4,2,1,3,0:T(8,128)(2,1)S(1)}, bf16[2,2,128,1,256]{4,2,1,3,0:T(8,128)(2,1)S(1)}, u32[]{:S(2)}, u32[]{:S(2)}) collective-permute-start(bf16[2,2,128,1,256]{4,2,1,3,0:T(8,128)(2,1)S(1)} %get-tuple-element.289), channel_id=1, source_target_pairs={{0,2},{2,0},{1,3},{3,1},{4,6},{6,4},{5,7},{7,5},{8,10},{10,8},{9,1... | collective-permute-start | bytes 786440 | tf_op jit(solution)/shard_map/ppermute | solution.py:17
  198.7 10.1 %collective-permute-start.14 = (bf16[2,2,128,1,256]{4,2,1,3,0:T(8,128)(2,1)S(1)}, bf16[2,2,128,1,256]{4,2,1,3,0:T(8,128)(2,1)S(1)}, u32[]{:S(2)}, u32[]{:S(2)}) collective-permute-start(bf16[2,2,128,1,256]{4,2,1,3,0:T(8,128)(2,1)S(1)} %get-tuple-element.269), channel_id=1, source_target_pairs={{0,2},{2,0},{1,3},{3,1},{4,6},{6,4},{5,7},{7,5},{8,10},{10,8},{9,1... | collective-permute-start | bytes 786440 | tf_op jit(solution)/shard_map/ppermute | solution.py:17
  202.6 12.4 %collective-permute-start.5 = (bf16[2,2,128,1,256]{4,2,1,3,0:T(8,128)(2,1)S(1)}, bf16[2,2,128,1,256]{4,2,1,3,0:T(8,128)(2,1)S(1)}, u32[]{:S(2)}, u32[]{:S(2)}) collective-permute-start(bf16[2,2,128,1,256]{4,2,1,3,0:T(8,128)(2,1)S(1)} %get-tuple-element.287), channel_id=1, source_target_pairs={{0,1},{1,0},{2,3},{3,2},{4,5},{5,4},{6,7},{7,6},{8,9},{9,8},{10,11... | collective-permute-start | bytes 786440 | tf_op jit(solution)/shard_map/ppermute | solution.py:17
  209.0 10.4 %collective-permute-start.15 = (bf16[2,2,128,1,256]{4,2,1,3,0:T(8,128)(2,1)S(1)}, bf16[2,2,128,1,256]{4,2,1,3,0:T(8,128)(2,1)S(1)}, u32[]{:S(2)}, u32[]{:S(2)}) collective-permute-start(bf16[2,2,128,1,256]{4,2,1,3,0:T(8,128)(2,1)S(1)} %get-tuple-element.267), channel_id=1, source_target_pairs={{0,1},{1,0},{2,3},{3,2},{4,5},{5,4},{6,7},{7,6},{8,9},{9,8},{10,11... | collective-permute-start | bytes 786440 | tf_op jit(solution)/shard_map/ppermute | solution.py:17
  229.5 7.1 %collective-permute-start.6 = (bf16[2,2,128,1,256]{4,2,1,3,0:T(8,128)(2,1)S(1)}, bf16[2,2,128,1,256]{4,2,1,3,0:T(8,128)(2,1)S(1)}, u32[]{:S(2)}, u32[]{:S(2)}) collective-permute-start(bf16[2,2,128,1,256]{4,2,1,3,0:T(8,128)(2,1)S(1)} %pad_maximum_fusion.5), channel_id=1, source_target_pairs={{0,1},{1,0},{2,3},{3,2},{4,5},{5,4},{6,7},{7,6},{8,9},{9,8},{10,11... | collective-permute-start | bytes 786440 | tf_op jit(solution)/shard_map/ppermute | solution.py:17
  236.9 9.2 %collective-permute-start.7 = (bf16[2,2,128,1,256]{4,2,1,3,0:T(8,128)(2,1)S(1)}, bf16[2,2,128,1,256]{4,2,1,3,0:T(8,128)(2,1)S(1)}, u32[]{:S(2)}, u32[]{:S(2)}) collective-permute-start(bf16[2,2,128,1,256]{4,2,1,3,0:T(8,128)(2,1)S(1)} %get-tuple-element.281), channel_id=1, source_target_pairs={{0,2},{2,0},{1,3},{3,1},{4,6},{6,4},{5,7},{7,5},{8,10},{10,8},{9,1... | collective-permute-start | bytes 786440 | tf_op jit(solution)/shard_map/ppermute | solution.py:17
  246.4 7.4 %collective-permute-start.8 = (bf16[2,2,128,1,256]{4,2,1,3,0:T(8,128)(2,1)S(1)}, bf16[2,2,128,1,256]{4,2,1,3,0:T(8,128)(2,1)S(1)}, u32[]{:S(2)}, u32[]{:S(2)}) collective-permute-start(bf16[2,2,128,1,256]{4,2,1,3,0:T(8,128)(2,1)S(1)} %get-tuple-element.279), channel_id=1, source_target_pairs={{0,4},{4,0},{1,5},{5,1},{2,6},{6,2},{3,7},{7,3},{8,12},{12,8},{9,1... | collective-permute-start | bytes 786440 | tf_op jit(solution)/shard_map/ppermute | solution.py:17
  254.1 11.5 %collective-permute-start.9 = (bf16[2,2,128,1,256]{4,2,1,3,0:T(8,128)(2,1)S(1)}, bf16[2,2,128,1,256]{4,2,1,3,0:T(8,128)(2,1)S(1)}, u32[]{:S(2)}, u32[]{:S(2)}) collective-permute-start(bf16[2,2,128,1,256]{4,2,1,3,0:T(8,128)(2,1)S(1)} %get-tuple-element.277), channel_id=1, source_target_pairs={{0,8},{8,0},{1,9},{9,1},{2,10},{10,2},{3,11},{11,3},{4,12},{12,4},... | collective-permute-start | bytes 786440 | tf_op jit(solution)/shard_map/ppermute | solution.py:17
  265.6 12.3 %copy-start.3 = (f32[128,256]{1,0:T(8,128)S(1)}, f32[128,256]{1,0:T(8,128)}, u32[]{:S(2)}) copy-start(f32[128,256]{1,0:T(8,128)} %copy-done.2) | copy-start | bytes 393220
  265.9 11.8 %collective-permute-start.10 = (bf16[2,2,128,1,256]{4,2,1,3,0:T(8,128)(2,1)S(1)}, bf16[2,2,128,1,256]{4,2,1,3,0:T(8,128)(2,1)S(1)}, u32[]{:S(2)}, u32[]{:S(2)}) collective-permute-start(bf16[2,2,128,1,256]{4,2,1,3,0:T(8,128)(2,1)S(1)} %get-tuple-element.275), channel_id=1, source_target_pairs={{0,16},{16,0},{1,17},{17,1},{2,18},{18,2},{3,19},{19,3},{4,20},{20... | collective-permute-start | bytes 786440 | tf_op jit(solution)/shard_map/ppermute | solution.py:17
  272.1 11.0 %collective-permute-start.16 = (bf16[2,2,128,1,256]{4,2,1,3,0:T(8,128)(2,1)S(1)}, bf16[2,2,128,1,256]{4,2,1,3,0:T(8,128)(2,1)S(1)}, u32[]{:S(2)}, u32[]{:S(2)}) collective-permute-start(bf16[2,2,128,1,256]{4,2,1,3,0:T(8,128)(2,1)S(1)} %pad_maximum_fusion.6), channel_id=1, source_target_pairs={{0,1},{1,0},{2,3},{3,2},{4,5},{5,4},{6,7},{7,6},{8,9},{9,8},{10,11... | collective-permute-start | bytes 786440 | tf_op jit(solution)/shard_map/ppermute | solution.py:17
  283.3 10.8 %collective-permute-start.17 = (bf16[2,2,128,1,256]{4,2,1,3,0:T(8,128)(2,1)S(1)}, bf16[2,2,128,1,256]{4,2,1,3,0:T(8,128)(2,1)S(1)}, u32[]{:S(2)}, u32[]{:S(2)}) collective-permute-start(bf16[2,2,128,1,256]{4,2,1,3,0:T(8,128)(2,1)S(1)} %get-tuple-element.261), channel_id=1, source_target_pairs={{0,2},{2,0},{1,3},{3,1},{4,6},{6,4},{5,7},{7,5},{8,10},{10,8},{9,1... | collective-permute-start | bytes 786440 | tf_op jit(solution)/shard_map/ppermute | solution.py:17
  294.4 7.8 %collective-permute-start.18 = (bf16[2,2,128,1,256]{4,2,1,3,0:T(8,128)(2,1)S(1)}, bf16[2,2,128,1,256]{4,2,1,3,0:T(8,128)(2,1)S(1)}, u32[]{:S(2)}, u32[]{:S(2)}) collective-permute-start(bf16[2,2,128,1,256]{4,2,1,3,0:T(8,128)(2,1)S(1)} %get-tuple-element.259), channel_id=1, source_target_pairs={{0,4},{4,0},{1,5},{5,1},{2,6},{6,2},{3,7},{7,3},{8,12},{12,8},{9,1... | collective-permute-start | bytes 786440 | tf_op jit(solution)/shard_map/ppermute | solution.py:17
  302.5 11.2 %collective-permute-start.19 = (bf16[2,2,128,1,256]{4,2,1,3,0:T(8,128)(2,1)S(1)}, bf16[2,2,128,1,256]{4,2,1,3,0:T(8,128)(2,1)S(1)}, u32[]{:S(2)}, u32[]{:S(2)}) collective-permute-start(bf16[2,2,128,1,256]{4,2,1,3,0:T(8,128)(2,1)S(1)} %get-tuple-element.257), channel_id=1, source_target_pairs={{0,8},{8,0},{1,9},{9,1},{2,10},{10,2},{3,11},{11,3},{4,12},{12,4},... | collective-permute-start | bytes 786440 | tf_op jit(solution)/shard_map/ppermute | solution.py:17
  313.9 46.7 %copy-start.1 = (bf16[128,8192]{1,0:T(8,128)(2,1)S(1)}, bf16[128,8192]{1,0:T(8,128)(2,1)}, u32[]{:S(2)}) copy-start(bf16[128,8192]{1,0:T(8,128)(2,1)} %param.13) | copy-start | bytes 6291460
  313.9 14.9 %collective-permute-start.20 = (bf16[2,2,128,1,256]{4,2,1,3,0:T(8,128)(2,1)S(1)}, bf16[2,2,128,1,256]{4,2,1,3,0:T(8,128)(2,1)S(1)}, u32[]{:S(2)}, u32[]{:S(2)}) collective-permute-start(bf16[2,2,128,1,256]{4,2,1,3,0:T(8,128)(2,1)S(1)} %get-tuple-element.255), channel_id=1, source_target_pairs={{0,16},{16,0},{1,17},{17,1},{2,18},{18,2},{3,19},{19,3},{4,20},{20... | collective-permute-start | bytes 786440 | tf_op jit(solution)/shard_map/ppermute | solution.py:17
  329.2 6.6 %collective-permute-start.21 = (f32[2,3,256]{2,0,1:T(2,128)S(1)}, f32[2,3,256]{2,0,1:T(2,128)S(1)}, u32[]{:S(2)}, u32[]{:S(2)}) collective-permute-start(f32[2,3,256]{2,0,1:T(2,128)S(1)} %slice.482), channel_id=1, source_target_pairs={{1,0},{2,1},{3,2},{4,3},{5,4},{6,5},{7,6},{8,7},{9,8},{10,9},{11,1... | collective-permute-start | bytes 18440 | tf_op jit(solution)/shard_map/ppermute | solution.py:23
Sparse Core Ops, SparseCore 0:
  283.1 77.4 reduce-scatter.1
